TPU v7x, 512 devices: a whole 4x8x8 slice. The times are simulated.
512 devices in a mesh: dp: 16 (over z_hi, x), seq: 32 (over y, z_lo, core).
Axes of the slice: x: 4, y: 8, z: 8 (z_hi: 4, z_lo: 2; z = z_hi * 2 + z_lo), core: 2. Of those that a mesh axis runs over, the one named last changes fastest.
Arguments:
- frame_features: bfloat16 [32, 4, 64, 32, 512], P('dp', None, 'seq'), may hold values from -6 to 6
- conv_weight: bfloat16 [27, 512, 32], replicated, may hold values from -0.0546875 to 0.0546875
- conv_bias: float32 [32], replicated, may hold values from -0.5 to 0.5
- vae_noise: float32 [32, 2048, 64], P('dp', 'seq'), may hold values from -6 to 6
- flow_noise: float32 [32, 2048, 64], P('dp', 'seq'), may hold values from -6 to 6
- head_queries: bfloat16 [32, 2048, 2048], P('dp', 'seq'), may hold values from -48 to 48
- head_keys: bfloat16 [32, 2048, 2048], P('dp', 'seq'), may hold values from -48 to 48
- head_values: bfloat16 [32, 2048, 2048], P('dp', 'seq'), may hold values from -6 to 6
- out_weight: bfloat16 [2048, 64], replicated, may hold values from -0.125 to 0.125
- out_bias: float32 [64], replicated, may hold values from -1 to 1
Outputs:
- grad_queries: bfloat16 [32, 2048, 2048], P('dp', 'seq')
- grad_keys: bfloat16 [32, 2048, 2048], P('dp', 'seq')
- grad_values: bfloat16 [32, 2048, 2048], P('dp', 'seq')
- grad_out_weight: float32 [2048, 64], P('seq')
All inputs are finite; a program needn't handle non-finite values.
Results may differ from a plain program's by a relative error of at most 0.019.
Values may be sent and summed in bfloat16 or wider, within the bound.
No kernel may reach another device: no remote copies, remote signals or barrier semaphores. Data moves between devices by JAX's collectives and lax.ppermute only.
A program may use at most 64 MiB of HBM per device.

v0:
```python
import math
import jax
import jax.numpy as jnp
from jax import lax
from jax.sharding import PartitionSpec as P

HEADS = 16
HDIM = 128
LATC = 16
latent_factor = 0.476986


def extended(x, sides, width):
    for axis, dim in sides:
        peers, length = (lax.axis_size(axis), x.shape[dim])
        up = [(i, (i + 1) % peers) for i in range(peers - 1)]
        down = [(j, i) for i, j in up]
        last = lax.slice_in_dim(x, length - width, length, axis=dim)
        leading = lax.slice_in_dim(x, 0, width, axis=dim)
        before = lax.ppermute(last, axis, up)
        after = lax.ppermute(leading, axis, down)
        x = jnp.concatenate([before, x, after], axis=dim)
    return x


def causal_conv(padded_rows, conv_weight, conv_bias):
    clip_count, frame_count, padded_height, column_count, channels = padded_rows.shape
    row_count = padded_height - 2
    opening = padded_rows[:, :1]
    timed = jnp.concatenate([opening, opening, padded_rows], axis=1)
    border = jnp.zeros((clip_count, frame_count + 2, padded_height, 1, channels), padded_rows.dtype)
    framed = jnp.concatenate([border, timed, border], axis=3)
    out_channels = conv_weight.shape[2]
    summed = jnp.zeros(
        (clip_count * frame_count * row_count * column_count, out_channels), jnp.float32
    )
    for frame_tap in range(3):
        for row_tap in range(3):
            for column_tap in range(3):
                window = framed[
                    :,
                    frame_tap : frame_tap + frame_count,
                    row_tap : row_tap + row_count,
                    column_tap : column_tap + column_count,
                ]
                summed = summed + jnp.dot(
                    window.reshape(-1, channels),
                    conv_weight[frame_tap * 9 + row_tap * 3 + column_tap],
                    preferred_element_type=jnp.float32,
                )
    summed = summed + conv_bias
    return summed.reshape(clip_count, frame_count, row_count, column_count, out_channels)


def to_tokens(grid):
    clip_count, frame_count, row_count, column_count, channels = grid.shape
    shaped = grid.reshape(
        clip_count, frame_count, row_count // 2, 2, column_count // 2, 2, channels
    )
    shaped = shaped.transpose(0, 2, 1, 4, 6, 3, 5)
    return shaped.reshape(
        clip_count, row_count // 2 * frame_count * (column_count // 2), channels * 4
    )


def make_target(encoded, vae_noise, flow_noise):
    mean_tokens = to_tokens(encoded[..., :LATC])
    logvar_tokens = to_tokens(encoded[..., LATC:])
    latent = mean_tokens + jnp.exp(0.5 * logvar_tokens) * vae_noise
    return flow_noise - latent_factor * latent


def to_pairs(token_array, head_blocks):
    clip_count, row_count, total_width = token_array.shape
    block_width = total_width // head_blocks
    shaped = token_array.reshape(clip_count, row_count, head_blocks, block_width).transpose(
        2, 0, 1, 3
    )
    return shaped.reshape(head_blocks * clip_count, row_count, block_width)


def from_pairs(received, clip_count):
    source_count, row_count, block_width = received.shape
    head_blocks = source_count // clip_count
    shaped = received.reshape(head_blocks, clip_count, row_count, block_width).transpose(1, 2, 0, 3)
    return shaped.reshape(clip_count, row_count, head_blocks * block_width)


def shards(
    frame_features,
    conv_weight,
    conv_bias,
    vae_noise,
    flow_noise,
    head_queries,
    head_keys,
    head_values,
    out_weight,
    out_bias,
):
    rank_count = lax.axis_size("seq")
    clip_count, dev_tokens, full_width = head_queries.shape
    feature_count = out_weight.shape[1]
    score_scale = 1.0 / math.sqrt(HDIM)
    activated = jax.nn.silu(frame_features.astype(jnp.float32)).astype(jnp.bfloat16)
    padded = extended(activated, (("seq", 2),), 1)
    encoded = causal_conv(padded, conv_weight, conv_bias)
    target = make_target(encoded, vae_noise, flow_noise)
    head_blocks = rank_count // clip_count
    pair_heads = clip_count * HEADS // rank_count
    pair_width = pair_heads * HDIM
    clip_rows = rank_count * dev_tokens
    block_rows = min(512, clip_rows)
    block_count = clip_rows // block_rows

    def forward_clip(query_piece, key_pair, value_pair):
        scores = (
            jnp.einsum("qhd,khd->hqk", query_piece, key_pair, preferred_element_type=jnp.float32)
            * score_scale
        )
        shifted = jnp.exp(scores - jnp.max(scores, axis=-1, keepdims=True))
        attn_probs = (shifted / jnp.sum(shifted, axis=-1, keepdims=True)).astype(jnp.bfloat16)
        attended = jnp.einsum(
            "hqk,khd->qhd", attn_probs, value_pair, preferred_element_type=jnp.float32
        ).astype(jnp.bfloat16)
        return (attn_probs, attended)

    got_queries, got_keys, got_values = (
        lax.all_to_all(
            to_pairs(head_queries, head_blocks), "seq", split_axis=0, concat_axis=0, tiled=True
        ),
        lax.all_to_all(
            to_pairs(head_keys, head_blocks), "seq", split_axis=0, concat_axis=0, tiled=True
        ),
        lax.all_to_all(
            to_pairs(head_values, head_blocks), "seq", split_axis=0, concat_axis=0, tiled=True
        ),
    )
    query_pair = got_queries.reshape(block_count, block_rows, pair_heads, HDIM)
    key_pair = got_keys.reshape(clip_rows, pair_heads, HDIM)
    value_pair = got_values.reshape(clip_rows, pair_heads, HDIM)

    def forward_block(query_piece):
        return forward_clip(query_piece, key_pair, value_pair)

    attn_probs, attended = lax.map(forward_block, query_pair)
    attended_flat = attended.reshape(clip_rows, pair_width)
    attended_back = lax.all_to_all(
        attended_flat.reshape(rank_count, dev_tokens, pair_width),
        "seq",
        split_axis=0,
        concat_axis=0,
        tiled=True,
    )
    attended_tokens = from_pairs(attended_back, clip_count).reshape(-1, full_width)
    predicted = jnp.dot(attended_tokens, out_weight, preferred_element_type=jnp.float32) + out_bias
    errors = (predicted.reshape(clip_count, dev_tokens, feature_count) - target).astype(
        jnp.bfloat16
    )
    errors_flat = errors.reshape(-1, feature_count)
    grad_tokens = jnp.einsum(
        "tp,wp->tw", errors_flat, out_weight, preferred_element_type=jnp.float32
    ).astype(jnp.bfloat16)
    grad_tokens = grad_tokens.reshape(clip_count, dev_tokens, full_width)
    grad_got = lax.all_to_all(
        to_pairs(grad_tokens, head_blocks), "seq", split_axis=0, concat_axis=0, tiled=True
    )
    grad_attended = grad_got.reshape(clip_rows, pair_width)
    weight_rows = lax.psum_scatter(
        jnp.einsum(
            "tw,tp->wp", attended_tokens, errors_flat, preferred_element_type=jnp.float32
        ).astype(jnp.bfloat16),
        "seq",
        scatter_dimension=0,
        tiled=True,
    ).astype(jnp.float32)
    grad_pair = grad_attended.reshape(block_count, block_rows, pair_heads, HDIM)

    def backward_block(carry, block_items):
        key_total, value_total = carry
        query_piece, probs_piece, attended_piece, grad_piece = block_items
        grad_probs = jnp.einsum(
            "qhd,khd->hqk", grad_piece, value_pair, preferred_element_type=jnp.float32
        )
        row_dots = jnp.sum(
            grad_piece.astype(jnp.float32) * attended_piece.astype(jnp.float32), axis=-1
        )
        grad_scores = (
            probs_piece.astype(jnp.float32) * (grad_probs - row_dots.T[:, :, None])
        ).astype(jnp.bfloat16)
        grad_query = (
            jnp.einsum("hqk,khd->qhd", grad_scores, key_pair, preferred_element_type=jnp.float32)
            * score_scale
        ).astype(jnp.bfloat16)
        key_part = (
            jnp.einsum("hqk,qhd->khd", grad_scores, query_piece, preferred_element_type=jnp.float32)
            * score_scale
        )
        value_part = jnp.einsum(
            "hqk,qhd->khd", probs_piece, grad_piece, preferred_element_type=jnp.float32
        )
        return ((key_total + key_part, value_total + value_part), grad_query)

    zero_total = jnp.zeros((clip_rows, pair_heads, HDIM), jnp.float32)
    totals, grad_query = lax.scan(
        backward_block, (zero_total, zero_total), (query_pair, attn_probs, attended, grad_pair)
    )
    query_send = grad_query.reshape(rank_count, dev_tokens, pair_width)
    key_send = totals[0].astype(jnp.bfloat16).reshape(rank_count, dev_tokens, pair_width)
    value_send = totals[1].astype(jnp.bfloat16).reshape(rank_count, dev_tokens, pair_width)
    query_back, key_back, value_back = (
        lax.all_to_all(query_send, "seq", split_axis=0, concat_axis=0, tiled=True),
        lax.all_to_all(key_send, "seq", split_axis=0, concat_axis=0, tiled=True),
        lax.all_to_all(value_send, "seq", split_axis=0, concat_axis=0, tiled=True),
    )
    grad_queries = from_pairs(query_back, clip_count)
    grad_keys = from_pairs(key_back, clip_count)
    grad_values = from_pairs(value_back, clip_count)
    grad_out_weight = lax.psum(weight_rows, "dp")
    return (grad_queries, grad_keys, grad_values, grad_out_weight)


def solution(mesh):
    return jax.shard_map(
        shards,
        mesh=mesh,
        in_specs=(
            P("dp", None, "seq", None, None),
            P(),
            P(),
            P("dp", "seq", None),
            P("dp", "seq", None),
            P("dp", "seq", None),
            P("dp", "seq", None),
            P("dp", "seq", None),
            P(),
            P(),
        ),
        out_specs=(
            P("dp", "seq", None),
            P("dp", "seq", None),
            P("dp", "seq", None),
            P("seq", None),
        ),
        check_vma=False,
    )
```

profile of v0, /device:TPU:32, one launch (start us, length us, event | category | flops | bytes accessed | tf_op | source)
XLA Modules:
  0.0 491.9 jit_solution(6019694938056784839)
XLA Ops:
  11.4 5.8 %collective-permute-start.1 = (bf16[2,4,1,32,512]{4,3,2,1,0:T(8,128)(2,1)S(1)}, bf16[2,4,1,32,512]{4,3,2,1,0:T(8,128)(2,1)S(1)}, u32[]{:S(2)}, u32[]{:S(2)}) collective-permute-start(bf16[2,4,1,32,512]{4,3,2,1,0:T(8,128)(2,1)S(1)} %get-tuple-element.234), channel_id=1, source_target_pairs={{1,0},{2,1},{3,2},{4,3},{5,4},{6,5},{7,6},{8,7},{9,8},{10,9},{11,1... | collective-permute-start | bytes 786440 | tf_op jit(solution)/shard_map/ppermute | solution.py:21
  18.1 7.4 %all-to-all-start = ((bf16[32,64,128]{2,1,0:T(8,128)(2,1)}), bf16[32,64,128]{2,1,0:T(8,128)(2,1)S(1)}, u32[]{:S(2)}, u32[]{:S(2)}) async-start(bf16[32,64,128]{2,1,0:T(8,128)(2,1)} %bitcast.9), calls=%async_computation | async-start | bytes 1048576 | tf_op jit(solution)/shard_map/all_to_all | solution.py:129
  33.3 5.8 %pad_slice_fusion.1 = (bf16[2,4,2,32,512]{4,3,2,1,0:T(8,128)(2,1)}, bf16[2,4,2,32,512]{4,3,2,1,0:T(8,128)(2,1)S(1)}, bf16[2,4,2,32,512]{4,3,2,1,0:T(8,128)(2,1)S...) fusion(bf16[2,6,4,32,512]{4,3,2,1,0:T(8,128)(2,1)S(1)} %maximum, ...), kind=kLoop, calls=%fused_computation.41 | loop fusion | bytes 12582912 | tf_op jit(solution)/shard_map/slice | solution.py:40
  53.4 8.3 %all-to-all-start.1 = ((bf16[32,64,128]{2,1,0:T(8,128)(2,1)}), bf16[32,64,128]{2,1,0:T(8,128)(2,1)S(1)}, u32[]{:S(2)}, u32[]{:S(2)}) async-start(bf16[32,64,128]{2,1,0:T(8,128)(2,1)} %bitcast.361), calls=%async_computation.1 | async-start | bytes 1048576 | tf_op jit(solution)/shard_map/all_to_all | solution.py:132
  68.1 7.1 %all-to-all-done.1 = bf16[32,64,128]{2,1,0:T(8,128)(2,1)S(1)} async-done(((bf16[32,64,128]{2,1,0:T(8,128)(2,1)}), bf16[32,64,128]{2,1,0:T(8,128)(2,1)S(1)}, u32[]{:S(2)}, u32[]{:S(2)}) %all-to-all-start.1) | async-done | bytes 524320 | tf_op jit(solution)/shard_map/all_to_all | solution.py:132
  75.1 8.8 %all-to-all-start.2 = ((bf16[32,64,128]{2,1,0:T(8,128)(2,1)}), bf16[32,64,128]{2,1,0:T(8,128)(2,1)}, u32[]{:S(2)}, u32[]{:S(2)}) async-start(bf16[32,64,128]{2,1,0:T(8,128)(2,1)} %bitcast.360), calls=%async_computation.2 | async-start | bytes 1048576 | tf_op jit(solution)/shard_map/all_to_all | solution.py:135
  91.7 5.8 %all-to-all-done.2 = bf16[32,64,128]{2,1,0:T(8,128)(2,1)} async-done(((bf16[32,64,128]{2,1,0:T(8,128)(2,1)}), bf16[32,64,128]{2,1,0:T(8,128)(2,1)}, u32[]{:S(2)}, u32[]{:S(2)}) %all-to-all-start.2) | async-done | bytes 524320 | tf_op jit(solution)/shard_map/all_to_all | solution.py:135
  98.3 28.8 %while.27 = (s32[]{:T(128)}, bf16[4,1,512,2048]{3,2,1,0:T(8,128)(2,1)}, bf16[4,512,1,128]{3,1,2,0:T(8,128)(2,1)}, bf16[4,512,1,128]{3,1,2,0:T(8,128)(2,1)}, bf16...) while((s32[]{:T(128)}, bf16[4,1,512,2048]{3,2,1,0:T(8,128)(2,1)}, ...), condition=%wide.region_3.4_spmd, body=%wide.region_0.3_spmd.sunk | while | flops 546372608 | bytes 20196940 | solution.py:146
  110.3 2.4 fusion.200
  124.7 2.4 fusion.200
  127.1 8.5 %all-to-all-start.3 = ((bf16[32,64,128]{2,1,0:T(8,128)(2,1)}), bf16[32,64,128]{2,1,0:T(8,128)(2,1)S(1)}, u32[]{:S(2)}, u32[]{:S(2)}) async-start(bf16[32,64,128]{2,1,0:T(8,128)(2,1)} %bitcast.19), calls=%async_computation.3 | async-start | bytes 1048576 | tf_op jit(solution)/shard_map/all_to_all | solution.py:148
  141.7 7.5 %all-to-all-done.3 = bf16[32,64,128]{2,1,0:T(8,128)(2,1)S(1)} async-done(((bf16[32,64,128]{2,1,0:T(8,128)(2,1)}), bf16[32,64,128]{2,1,0:T(8,128)(2,1)S(1)}, u32[]{:S(2)}, u32[]{:S(2)}) %all-to-all-start.3) | async-done | bytes 524320 | tf_op jit(solution)/shard_map/all_to_all | solution.py:148
  152.3 8.4 %all-to-all-start.4 = ((bf16[32,64,128]{2,1,0:T(8,128)(2,1)}), bf16[32,64,128]{2,1,0:T(8,128)(2,1)S(1)}, u32[]{:S(2)}, u32[]{:S(2)}) async-start(bf16[32,64,128]{2,1,0:T(8,128)(2,1)} %bitcast.81), calls=%async_computation.4 | async-start | bytes 1048576 | tf_op jit(solution)/shard_map/all_to_all | solution.py:165
  160.7 13.5 %all-to-all-done.4 = bf16[32,64,128]{2,1,0:T(8,128)(2,1)S(1)} async-done(((bf16[32,64,128]{2,1,0:T(8,128)(2,1)}), bf16[32,64,128]{2,1,0:T(8,128)(2,1)S(1)}, u32[]{:S(2)}, u32[]{:S(2)}) %all-to-all-start.4) | async-done | bytes 524320 | tf_op jit(solution)/shard_map/all_to_all | solution.py:165
  175.0 44.6 %while.28 = (s32[]{:T(128)}, f32[2048,1,128]{0,2,1:T(8,128)}, f32[2048,1,128]{0,2,1:T(8,128)}, bf16[4,512,1,128]{3,1,2,0:T(8,128)(2,1)}, bf16[4,512,1,128]{3,1,2...) while((s32[]{:T(128)}, f32[2048,1,128]{0,2,1:T(8,128)}, ...), condition=%wide.region_6.7_spmd.clone, body=%wide.region_4.6_spmd.clone.sunk | while | flops 1079639552 | bytes 20716732 | solution.py:205
  176.2 2.5 multiply_convert_fusion.2
  182.5 3.2 fusion.210
  186.9 2.5 multiply_convert_fusion.2
  189.4 2.8 fusion.209
  193.5 3.4 fusion.210
  198.2 2.5 multiply_convert_fusion.2
  200.7 2.8 fusion.209
  204.9 3.4 fusion.210
  209.5 2.5 multiply_convert_fusion.2
  212.0 2.8 fusion.209
  216.2 3.4 fusion.210
  221.9 8.4 %all-to-all-start.7 = ((bf16[32,64,128]{2,1,0:T(8,128)(2,1)}), bf16[32,64,128]{2,1,0:T(8,128)(2,1)S(1)}, u32[]{:S(2)}, u32[]{:S(2)}) async-start(bf16[32,64,128]{2,1,0:T(8,128)(2,1)} %bitcast.90), calls=%async_computation.7 | async-start | bytes 1048576 | tf_op jit(solution)/shard_map/all_to_all | solution.py:214
  230.6 13.2 %all-to-all-done.7 = bf16[32,64,128]{2,1,0:T(8,128)(2,1)S(1)} async-done(((bf16[32,64,128]{2,1,0:T(8,128)(2,1)}), bf16[32,64,128]{2,1,0:T(8,128)(2,1)S(1)}, u32[]{:S(2)}, u32[]{:S(2)}) %all-to-all-start.7) | async-done | bytes 524320 | tf_op jit(solution)/shard_map/all_to_all | solution.py:214
  243.8 20.9 %all_to_all.40 = bf16[32,64,128]{2,1,0:T(8,128)(2,1)S(1)} all-to-all(bf16[32,64,128]{2,1,0:T(8,128)(2,1)S(1)} %bitcast.357), channel_id=1, replica_groups=mesh['dp'=16,'seq'=32] {'seq'}, dimensions={0} | all-to-all | bytes 1048576 | tf_op jit(solution)/shard_map/all_to_all | solution.py:213
  264.7 8.4 %all-to-all-start.5 = ((bf16[32,64,128]{2,1,0:T(8,128)(2,1)}), bf16[32,64,128]{2,1,0:T(8,128)(2,1)S(1)}, u32[]{:S(2)}, u32[]{:S(2)}) async-start(bf16[32,64,128]{2,1,0:T(8,128)(2,1)} %bitcast.366), calls=%async_computation.5 | async-start | bytes 1048576 | tf_op jit(solution)/shard_map/all_to_all | solution.py:212
  274.3 124.8 %reduce-scatter.2.cloned.1.call-done = bf16[64,64]{1,0:T(8,128)(2,1)} async-done(((bf16[2048,64]{1,0:T(8,128)(2,1)}), bf16[64,64]{1,0:T(8,128)(2,1)}) %reduce-scatter.2.cloned.1.call-update) | async-done | bytes 8208 | tf_op jit(solution)/shard_map/reduce_scatter | solution.py:169
  399.1 83.1 %psum.7 = f32[64,64]{1,0:T(8,128)} all-reduce(bf16[64,64]{1,0:T(8,128)(2,1)} %reduce-scatter.2.cloned.1.call-done), channel_id=1, replica_groups=mesh['dp'=16,'seq'=32] {'dp'}, use_global_device_ids=true, to_apply=%region_8.9 | all-reduce | flops 4096 | bytes 24576 | tf_op jit(solution)/shard_map/psum | solution.py:219
  (162 shorter events, 95.1 us)
Async XLA Ops:
  7.2 10.0 %copy-start = (bf16[2,64,2048]{2,1,0:T(8,128)(2,1)S(1)}, bf16[2,64,2048]{2,1,0:T(8,128)(2,1)}, u32[]{:S(2)}) copy-start(bf16[2,64,2048]{2,1,0:T(8,128)(2,1)} %param.19) | copy-start | bytes 1572868
  7.2 18.3 %copy-start.14 = (bf16[2,64,2048]{2,1,0:T(8,128)(2,1)S(1)}, bf16[2,64,2048]{2,1,0:T(8,128)(2,1)}, u32[]{:S(2)}) copy-start(bf16[2,64,2048]{2,1,0:T(8,128)(2,1)} %param.20) | copy-start | bytes 1572868
  9.4 18.1 %copy-start.24 = (f32[2,64,64]{2,1,0:T(8,128)S(1)}, f32[2,64,64]{2,1,0:T(8,128)}, u32[]{:S(2)}) copy-start(f32[2,64,64]{2,1,0:T(8,128)} %param.17) | copy-start | bytes 98308
  9.4 20.4 %copy-start.15 = (bf16[2,64,2048]{2,1,0:T(8,128)(2,1)S(1)}, bf16[2,64,2048]{2,1,0:T(8,128)(2,1)}, u32[]{:S(2)}) copy-start(bf16[2,64,2048]{2,1,0:T(8,128)(2,1)} %param.21) | copy-start | bytes 1572868
  9.4 21.3 %collective-permute-start = (bf16[2,4,1,32,512]{4,3,2,1,0:T(8,128)(2,1)}, bf16[2,4,1,32,512]{4,3,2,1,0:T(8,128)(2,1)S(1)}, u32[]{:S(2)}, u32[]{:S(2)}) collective-permute-start(bf16[2,4,1,32,512]{4,3,2,1,0:T(8,128)(2,1)} %get-tuple-element.233), channel_id=1, source_target_pairs={{0,1},{1,2},{2,3},{3,4},{4,5},{5,6},{6,7},{7,8},{8,9},{9,10},{10,1... | collective-permute-start | bytes 786440 | tf_op jit(solution)/shard_map/ppermute | solution.py:20
  11.4 19.3 %collective-permute-start.1 = (bf16[2,4,1,32,512]{4,3,2,1,0:T(8,128)(2,1)S(1)}, bf16[2,4,1,32,512]{4,3,2,1,0:T(8,128)(2,1)S(1)}, u32[]{:S(2)}, u32[]{:S(2)}) collective-permute-start(bf16[2,4,1,32,512]{4,3,2,1,0:T(8,128)(2,1)S(1)} %get-tuple-element.234), channel_id=1, source_target_pairs={{1,0},{2,1},{3,2},{4,3},{5,4},{6,5},{7,6},{8,7},{9,8},{10,9},{11,1... | collective-permute-start | bytes 786440 | tf_op jit(solution)/shard_map/ppermute | solution.py:21
  18.1 34.5 %all-to-all-start = ((bf16[32,64,128]{2,1,0:T(8,128)(2,1)}), bf16[32,64,128]{2,1,0:T(8,128)(2,1)S(1)}, u32[]{:S(2)}, u32[]{:S(2)}) async-start(bf16[32,64,128]{2,1,0:T(8,128)(2,1)} %bitcast.9), calls=%async_computation | async-start | bytes 1048576 | tf_op jit(solution)/shard_map/all_to_all | solution.py:129
  33.3 5.8 %copy-start.13 = (bf16[27,512,32]{1,2,0:T(8,128)(2,1)S(1)}, bf16[27,512,32]{1,2,0:T(8,128)(2,1)}, u32[]{:S(2)}) copy-start(bf16[27,512,32]{1,2,0:T(8,128)(2,1)} %param.15) | copy-start | bytes 2654212
  53.4 21.7 %all-to-all-start.1 = ((bf16[32,64,128]{2,1,0:T(8,128)(2,1)}), bf16[32,64,128]{2,1,0:T(8,128)(2,1)S(1)}, u32[]{:S(2)}, u32[]{:S(2)}) async-start(bf16[32,64,128]{2,1,0:T(8,128)(2,1)} %bitcast.361), calls=%async_computation.1 | async-start | bytes 1048576 | tf_op jit(solution)/shard_map/all_to_all | solution.py:132
  75.1 22.3 %all-to-all-start.2 = ((bf16[32,64,128]{2,1,0:T(8,128)(2,1)}), bf16[32,64,128]{2,1,0:T(8,128)(2,1)}, u32[]{:S(2)}, u32[]{:S(2)}) async-start(bf16[32,64,128]{2,1,0:T(8,128)(2,1)} %bitcast.360), calls=%async_computation.2 | async-start | bytes 1048576 | tf_op jit(solution)/shard_map/all_to_all | solution.py:135
  85.7 4.3 copy-start.9
  98.3 37.3 %copy-start.8 = (bf16[2,4,2,32,512]{4,3,2,1,0:T(8,128)(2,1)S(1)}, bf16[2,4,2,32,512]{4,3,2,1,0:T(8,128)(2,1)}, u32[]{:S(2)}) copy-start(bf16[2,4,2,32,512]{4,3,2,1,0:T(8,128)(2,1)} %get-tuple-element.215) | copy-start | bytes 1572868
  98.3 38.4 %copy-start.12 = (bf16[2,4,2,32,512]{4,3,2,1,0:T(8,128)(2,1)S(1)}, bf16[2,4,2,32,512]{4,3,2,1,0:T(8,128)(2,1)}, u32[]{:S(2)}) copy-start(bf16[2,4,2,32,512]{4,3,2,1,0:T(8,128)(2,1)} %get-tuple-element.232) | copy-start | bytes 1572868
  127.1 10.6 %copy-start.17 = (f32[512,32]{0,1:T(8,128)S(1)}, f32[512,32]{0,1:T(8,128)}, u32[]{:S(2)}) copy-start(f32[512,32]{0,1:T(8,128)} %fusion.103) | copy-start | bytes 196612
  127.1 10.7 %copy-start.18 = (f32[512,32]{0,1:T(8,128)S(1)}, f32[512,32]{0,1:T(8,128)}, u32[]{:S(2)}) copy-start(f32[512,32]{0,1:T(8,128)} %fusion.105) | copy-start | bytes 196612
  127.1 10.7 %copy-start.19 = (f32[512,32]{0,1:T(8,128)S(1)}, f32[512,32]{0,1:T(8,128)}, u32[]{:S(2)}) copy-start(f32[512,32]{0,1:T(8,128)} %fusion.107) | copy-start | bytes 196612
  127.1 10.7 %copy-start.20 = (f32[512,32]{0,1:T(8,128)S(1)}, f32[512,32]{0,1:T(8,128)}, u32[]{:S(2)}) copy-start(f32[512,32]{0,1:T(8,128)} %fusion.109) | copy-start | bytes 196612
  127.1 12.4 %copy-start.7 = (bf16[2,4,2,32,512]{4,3,2,1,0:T(8,128)(2,1)S(1)}, bf16[2,4,2,32,512]{4,3,2,1,0:T(8,128)(2,1)}, u32[]{:S(2)}) copy-start(bf16[2,4,2,32,512]{4,3,2,1,0:T(8,128)(2,1)} %get-tuple-element.207) | copy-start | bytes 1572868
  127.1 12.4 %copy-start.25 = (f32[32]{0:T(128)S(1)}, f32[32]{0:T(128)}, u32[]{:S(2)}) copy-start(f32[32]{0:T(128)} %param.16) | copy-start | bytes 388
  127.1 22.0 %all-to-all-start.3 = ((bf16[32,64,128]{2,1,0:T(8,128)(2,1)}), bf16[32,64,128]{2,1,0:T(8,128)(2,1)S(1)}, u32[]{:S(2)}, u32[]{:S(2)}) async-start(bf16[32,64,128]{2,1,0:T(8,128)(2,1)} %bitcast.19), calls=%async_computation.3 | async-start | bytes 1048576 | tf_op jit(solution)/shard_map/all_to_all | solution.py:148
  135.7 3.9 copy-start.21
  140.6 9.7 %copy-start.16 = (bf16[2048,64]{0,1:T(8,128)(2,1)S(1)}, bf16[2048,64]{0,1:T(8,128)(2,1)}, u32[]{:S(2)}) copy-start(bf16[2048,64]{0,1:T(8,128)(2,1)} %param.22) | copy-start | bytes 786436
  140.6 9.7 %copy-start.26 = (f32[64]{0:T(128)S(1)}, f32[64]{0:T(128)}, u32[]{:S(2)}) copy-start(f32[64]{0:T(128)} %param.23) | copy-start | bytes 772
  140.9 9.8 %copy-start.22 = (f32[2,64,64]{1,2,0:T(8,128)S(1)}, f32[2,64,64]{1,2,0:T(8,128)}, u32[]{:S(2)}) copy-start(f32[2,64,64]{1,2,0:T(8,128)} %copy.46) | copy-start | bytes 98308
  140.9 9.8 %copy-start.23 = (f32[2,64,64]{1,2,0:T(8,128)S(1)}, f32[2,64,64]{1,2,0:T(8,128)}, u32[]{:S(2)}) copy-start(f32[2,64,64]{1,2,0:T(8,128)} %copy.47) | copy-start | bytes 98308
  152.3 21.9 %all-to-all-start.4 = ((bf16[32,64,128]{2,1,0:T(8,128)(2,1)}), bf16[32,64,128]{2,1,0:T(8,128)(2,1)S(1)}, u32[]{:S(2)}, u32[]{:S(2)}) async-start(bf16[32,64,128]{2,1,0:T(8,128)(2,1)} %bitcast.81), calls=%async_computation.4 | async-start | bytes 1048576 | tf_op jit(solution)/shard_map/all_to_all | solution.py:165
  216.2 3.4 copy-start.3
  219.6 10.7 %copy-start.1 = (f32[2048,1,128]{0,2,1:T(8,128)S(1)}, f32[2048,1,128]{0,2,1:T(8,128)}, u32[]{:S(2)}) copy-start(f32[2048,1,128]{0,2,1:T(8,128)} %get-tuple-element.94) | copy-start | bytes 3145732
  221.9 21.9 %all-to-all-start.7 = ((bf16[32,64,128]{2,1,0:T(8,128)(2,1)}), bf16[32,64,128]{2,1,0:T(8,128)(2,1)S(1)}, u32[]{:S(2)}, u32[]{:S(2)}) async-start(bf16[32,64,128]{2,1,0:T(8,128)(2,1)} %bitcast.90), calls=%async_computation.7 | async-start | bytes 1048576 | tf_op jit(solution)/shard_map/all_to_all | solution.py:214
  230.3 42.9 %copy-start.11 = (bf16[2,64,16,128]{3,2,1,0:T(8,128)(2,1)S(1)}, bf16[2,64,16,128]{3,2,1,0:T(8,128)(2,1)}, u32[]{:S(2)}) copy-start(bf16[2,64,16,128]{3,2,1,0:T(8,128)(2,1)} %copy-done.10) | copy-start | bytes 1572868
  264.7 219.4 %all-to-all-start.5 = ((bf16[32,64,128]{2,1,0:T(8,128)(2,1)}), bf16[32,64,128]{2,1,0:T(8,128)(2,1)S(1)}, u32[]{:S(2)}, u32[]{:S(2)}) async-start(bf16[32,64,128]{2,1,0:T(8,128)(2,1)} %bitcast.366), calls=%async_computation.5 | async-start | bytes 1048576 | tf_op jit(solution)/shard_map/all_to_all | solution.py:212
  273.1 126.0 %reduce-scatter.2.cloned.1.call-start = ((), (), s32[]{:S(2)}) async-start(), calls=%async_computation.9 | async-start | bytes 540672 | tf_op jit(solution)/shard_map/reduce_scatter | solution.py:169
  (11 other events, 17.8 us)
Sparse Core Ops, SparseCore 0:
  277.3 121.8 reduce-scatter.1
where the time goes:
time: 494 us; the launch traced here: 492 us
  waiting for transfers between devices  172 us (35%)
  blocking collectives  104 us (21%)
  matrix products  87.2 us (18%)
  starting transfers between devices  65.9 us (13%)
  local copies, waits for them, and re-layouts  25.5 us (5%)
  other arithmetic  22.8 us (5%)
  between operations  14.5 us (3%)
    reduce_scatter x1, waiting for transfers between devices, shards(): lax.psum_scatter(jnp.einsum('tw,tp->wp', attended_tokens, errors_flat, pr...  125 us
    psum x1, blocking collectives, shards(): grad_out_weight = lax.psum(weight_rows, 'dp')  83.1 us
    dot_general x27, matrix products, causal_conv(): jnp.dot(window.reshape(-1, channels), conv_weight[frame_tap * 9 + row_tap...  29.2 us
    all_to_all x1, blocking collectives, shards(): lax.all_to_all(key_send, 'seq', split_axis=0, concat_axis=0, tiled=True)  20.9 us
    dot_general x4, matrix products, backward_block(): jnp.einsum('hqk,qhd->khd', probs_piece, grad_piece, preferred_element_typ...  13.5 us
    all_to_all x1, waiting for transfers between devices, shards(): lax.all_to_all(to_pairs(grad_tokens, head_blocks), 'seq', split_axis=0, c...  13.5 us
    all_to_all x1, waiting for transfers between devices, shards(): lax.all_to_all(value_send, 'seq', split_axis=0, concat_axis=0, tiled=True)  13.2 us
    dot_general x4, matrix products, backward_block(): jnp.einsum('hqk,qhd->khd', grad_scores, query_piece, preferred_element_ty...  10.7 us
  transfers between devices with their start and end apart: 10, of which 6 were waited for; matrix products, arithmetic and copies ran while one was open for 10% of the time, Pallas kernels for 0%

commit v1 on v0

--- a/solution.py
+++ b/solution.py
@@ -216,7 +216,7 @@
     grad_queries = from_pairs(query_back, clip_count)
     grad_keys = from_pairs(key_back, clip_count)
     grad_values = from_pairs(value_back, clip_count)
-    grad_out_weight = lax.psum(weight_rows, "dp")
+    grad_out_weight = jnp.sum(lax.all_gather(weight_rows, "dp"), axis=0)
     return (grad_queries, grad_keys, grad_values, grad_out_weight)
 
 

time: 494 us -> 460 us (0.931)
  blocking collectives: 104 us -> 68.6 us
    psum x1 -> x0, blocking collectives: 83.1 us -> none  [shards(): grad_out_weight = lax.psum(weight_rows, 'dp')]
    all_gather x0 -> x1, blocking collectives: none -> 47.7 us  [shards(): grad_out_weight = jnp.sum(lax.all_gather(weight_rows, 'dp'), axis=0)]
  transfers between devices with their start and end apart: 10 -> 10, of which waited for: 6 -> 6; matrix products, arithmetic and copies ran while one was open for 10% -> 11% of each run, Pallas kernels for 0% -> 0%
where the time goes in v1:
time: 460 us; the launch traced here: 458 us
  waiting for transfers between devices  172 us (37%)
  matrix products  87.2 us (19%)
  blocking collectives  68.6 us (15%)
  starting transfers between devices  65.9 us (14%)
  local copies, waits for them, and re-layouts  25.5 us (6%)
  other arithmetic  24.1 us (5%)
  between operations  14.5 us (3%)
    reduce_scatter x1, waiting for transfers between devices, shards(): lax.psum_scatter(jnp.einsum('tw,tp->wp', attended_tokens, errors_flat, pr...  125 us
    all_gather x1, blocking collectives, shards(): grad_out_weight = jnp.sum(lax.all_gather(weight_rows, 'dp'), axis=0)  47.7 us
    dot_general x27, matrix products, causal_conv(): jnp.dot(window.reshape(-1, channels), conv_weight[frame_tap * 9 + row_tap...  29.2 us
    all_to_all x1, blocking collectives, shards(): lax.all_to_all(key_send, 'seq', split_axis=0, concat_axis=0, tiled=True)  20.9 us
    dot_general x4, matrix products, backward_block(): jnp.einsum('hqk,qhd->khd', probs_piece, grad_piece, preferred_element_typ...  13.5 us
    all_to_all x1, waiting for transfers between devices, shards(): lax.all_to_all(to_pairs(grad_tokens, head_blocks), 'seq', split_axis=0, c...  13.5 us
    all_to_all x1, waiting for transfers between devices, shards(): lax.all_to_all(value_send, 'seq', split_axis=0, concat_axis=0, tiled=True)  13.2 us
    dot_general x4, matrix products, backward_block(): jnp.einsum('hqk,qhd->khd', grad_scores, query_piece, preferred_element_ty...  10.7 us
  transfers between devices with their start and end apart: 10, of which 6 were waited for; matrix products, arithmetic and copies ran while one was open for 11% of the time, Pallas kernels for 0%

profile of v1, /device:TPU:32, one launch (start us, length us, event | category | flops | bytes accessed | tf_op | source)
XLA Modules:
  0.0 457.9 jit_solution(9751328518874144720)
XLA Ops:
  11.4 5.8 %collective-permute-start.1 = (bf16[2,4,1,32,512]{4,3,2,1,0:T(8,128)(2,1)S(1)}, bf16[2,4,1,32,512]{4,3,2,1,0:T(8,128)(2,1)S(1)}, u32[]{:S(2)}, u32[]{:S(2)}) collective-permute-start(bf16[2,4,1,32,512]{4,3,2,1,0:T(8,128)(2,1)S(1)} %get-tuple-element.234), channel_id=1, source_target_pairs={{1,0},{2,1},{3,2},{4,3},{5,4},{6,5},{7,6},{8,7},{9,8},{10,9},{11,1... | collective-permute-start | bytes 786440 | tf_op jit(solution)/shard_map/ppermute | solution.py:21
  18.1 7.4 %all-to-all-start = ((bf16[32,64,128]{2,1,0:T(8,128)(2,1)}), bf16[32,64,128]{2,1,0:T(8,128)(2,1)S(1)}, u32[]{:S(2)}, u32[]{:S(2)}) async-start(bf16[32,64,128]{2,1,0:T(8,128)(2,1)} %bitcast.9), calls=%async_computation | async-start | bytes 1048576 | tf_op jit(solution)/shard_map/all_to_all | solution.py:129
  33.3 5.8 %pad_slice_fusion.1 = (bf16[2,4,2,32,512]{4,3,2,1,0:T(8,128)(2,1)}, bf16[2,4,2,32,512]{4,3,2,1,0:T(8,128)(2,1)S(1)}, bf16[2,4,2,32,512]{4,3,2,1,0:T(8,128)(2,1)S...) fusion(bf16[2,6,4,32,512]{4,3,2,1,0:T(8,128)(2,1)S(1)} %maximum, ...), kind=kLoop, calls=%fused_computation.41 | loop fusion | bytes 12582912 | tf_op jit(solution)/shard_map/slice | solution.py:40
  53.4 8.3 %all-to-all-start.1 = ((bf16[32,64,128]{2,1,0:T(8,128)(2,1)}), bf16[32,64,128]{2,1,0:T(8,128)(2,1)S(1)}, u32[]{:S(2)}, u32[]{:S(2)}) async-start(bf16[32,64,128]{2,1,0:T(8,128)(2,1)} %bitcast.363), calls=%async_computation.1 | async-start | bytes 1048576 | tf_op jit(solution)/shard_map/all_to_all | solution.py:132
  68.1 7.1 %all-to-all-done.1 = bf16[32,64,128]{2,1,0:T(8,128)(2,1)S(1)} async-done(((bf16[32,64,128]{2,1,0:T(8,128)(2,1)}), bf16[32,64,128]{2,1,0:T(8,128)(2,1)S(1)}, u32[]{:S(2)}, u32[]{:S(2)}) %all-to-all-start.1) | async-done | bytes 524320 | tf_op jit(solution)/shard_map/all_to_all | solution.py:132
  75.1 8.8 %all-to-all-start.2 = ((bf16[32,64,128]{2,1,0:T(8,128)(2,1)}), bf16[32,64,128]{2,1,0:T(8,128)(2,1)}, u32[]{:S(2)}, u32[]{:S(2)}) async-start(bf16[32,64,128]{2,1,0:T(8,128)(2,1)} %bitcast.362), calls=%async_computation.2 | async-start | bytes 1048576 | tf_op jit(solution)/shard_map/all_to_all | solution.py:135
  91.7 5.8 %all-to-all-done.2 = bf16[32,64,128]{2,1,0:T(8,128)(2,1)} async-done(((bf16[32,64,128]{2,1,0:T(8,128)(2,1)}), bf16[32,64,128]{2,1,0:T(8,128)(2,1)}, u32[]{:S(2)}, u32[]{:S(2)}) %all-to-all-start.2) | async-done | bytes 524320 | tf_op jit(solution)/shard_map/all_to_all | solution.py:135
  98.3 28.8 %while.27 = (s32[]{:T(128)}, bf16[4,1,512,2048]{3,2,1,0:T(8,128)(2,1)}, bf16[4,512,1,128]{3,1,2,0:T(8,128)(2,1)}, bf16[4,512,1,128]{3,1,2,0:T(8,128)(2,1)}, bf16...) while((s32[]{:T(128)}, bf16[4,1,512,2048]{3,2,1,0:T(8,128)(2,1)}, ...), condition=%wide.region_3.4_spmd, body=%wide.region_0.3_spmd.sunk | while | flops 546372608 | bytes 20196940 | solution.py:146
  110.3 2.4 fusion.200
  124.7 2.4 fusion.200
  127.1 8.5 %all-to-all-start.3 = ((bf16[32,64,128]{2,1,0:T(8,128)(2,1)}), bf16[32,64,128]{2,1,0:T(8,128)(2,1)S(1)}, u32[]{:S(2)}, u32[]{:S(2)}) async-start(bf16[32,64,128]{2,1,0:T(8,128)(2,1)} %bitcast.19), calls=%async_computation.3 | async-start | bytes 1048576 | tf_op jit(solution)/shard_map/all_to_all | solution.py:148
  141.7 7.5 %all-to-all-done.3 = bf16[32,64,128]{2,1,0:T(8,128)(2,1)S(1)} async-done(((bf16[32,64,128]{2,1,0:T(8,128)(2,1)}), bf16[32,64,128]{2,1,0:T(8,128)(2,1)S(1)}, u32[]{:S(2)}, u32[]{:S(2)}) %all-to-all-start.3) | async-done | bytes 524320 | tf_op jit(solution)/shard_map/all_to_all | solution.py:148
  152.3 8.4 %all-to-all-start.4 = ((bf16[32,64,128]{2,1,0:T(8,128)(2,1)}), bf16[32,64,128]{2,1,0:T(8,128)(2,1)S(1)}, u32[]{:S(2)}, u32[]{:S(2)}) async-start(bf16[32,64,128]{2,1,0:T(8,128)(2,1)} %bitcast.81), calls=%async_computation.4 | async-start | bytes 1048576 | tf_op jit(solution)/shard_map/all_to_all | solution.py:165
  160.7 13.5 %all-to-all-done.4 = bf16[32,64,128]{2,1,0:T(8,128)(2,1)S(1)} async-done(((bf16[32,64,128]{2,1,0:T(8,128)(2,1)}), bf16[32,64,128]{2,1,0:T(8,128)(2,1)S(1)}, u32[]{:S(2)}, u32[]{:S(2)}) %all-to-all-start.4) | async-done | bytes 524320 | tf_op jit(solution)/shard_map/all_to_all | solution.py:165
  175.0 44.6 %while.28 = (s32[]{:T(128)}, f32[2048,1,128]{0,2,1:T(8,128)}, f32[2048,1,128]{0,2,1:T(8,128)}, bf16[4,512,1,128]{3,1,2,0:T(8,128)(2,1)}, bf16[4,512,1,128]{3,1,2...) while((s32[]{:T(128)}, f32[2048,1,128]{0,2,1:T(8,128)}, ...), condition=%wide.region_6.7_spmd.clone, body=%wide.region_4.6_spmd.clone.sunk | while | flops 1079639552 | bytes 20716732 | solution.py:205
  176.2 2.5 multiply_convert_fusion.2
  182.5 3.2 fusion.210
  186.9 2.5 multiply_convert_fusion.2
  189.4 2.8 fusion.209
  193.6 3.4 fusion.210
  198.2 2.5 multiply_convert_fusion.2
  200.7 2.8 fusion.209
  204.9 3.4 fusion.210
  209.5 2.5 multiply_convert_fusion.2
  212.0 2.8 fusion.209
  216.2 3.4 fusion.210
  221.9 8.4 %all-to-all-start.7 = ((bf16[32,64,128]{2,1,0:T(8,128)(2,1)}), bf16[32,64,128]{2,1,0:T(8,128)(2,1)S(1)}, u32[]{:S(2)}, u32[]{:S(2)}) async-start(bf16[32,64,128]{2,1,0:T(8,128)(2,1)} %bitcast.90), calls=%async_computation.7 | async-start | bytes 1048576 | tf_op jit(solution)/shard_map/all_to_all | solution.py:214
  230.6 13.2 %all-to-all-done.7 = bf16[32,64,128]{2,1,0:T(8,128)(2,1)S(1)} async-done(((bf16[32,64,128]{2,1,0:T(8,128)(2,1)}), bf16[32,64,128]{2,1,0:T(8,128)(2,1)S(1)}, u32[]{:S(2)}, u32[]{:S(2)}) %all-to-all-start.7) | async-done | bytes 524320 | tf_op jit(solution)/shard_map/all_to_all | solution.py:214
  243.8 20.9 %all_to_all.40 = bf16[32,64,128]{2,1,0:T(8,128)(2,1)S(1)} all-to-all(bf16[32,64,128]{2,1,0:T(8,128)(2,1)S(1)} %bitcast.358), channel_id=1, replica_groups=mesh['dp'=16,'seq'=32] {'seq'}, dimensions={0} | all-to-all | bytes 1048576 | tf_op jit(solution)/shard_map/all_to_all | solution.py:213
  264.7 8.4 %all-to-all-start.5 = ((bf16[32,64,128]{2,1,0:T(8,128)(2,1)}), bf16[32,64,128]{2,1,0:T(8,128)(2,1)S(1)}, u32[]{:S(2)}, u32[]{:S(2)}) async-start(bf16[32,64,128]{2,1,0:T(8,128)(2,1)} %bitcast.368), calls=%async_computation.5 | async-start | bytes 1048576 | tf_op jit(solution)/shard_map/all_to_all | solution.py:212
  274.3 124.8 %reduce-scatter.2.cloned.1.call-done = bf16[64,64]{1,0:T(8,128)(2,1)} async-done(((bf16[2048,64]{1,0:T(8,128)(2,1)}), bf16[64,64]{1,0:T(8,128)(2,1)}) %reduce-scatter.2.cloned.1.call-update) | async-done | bytes 8208 | tf_op jit(solution)/shard_map/reduce_scatter | solution.py:169
  399.9 47.7 %all-gather = f32[1024,64]{1,0:T(8,128)S(1)} all-gather(f32[64,64]{1,0:T(8,128)S(1)} %all_gather.12), channel_id=2, replica_groups=mesh['dp'=16,'seq'=32] {'dp'}, dimensions={0}, use_global_device_ids=true | all-gather | bytes 278528 | tf_op jit(solution)/shard_map/all_gather | solution.py:219
  (164 shorter events, 96.5 us)
Async XLA Ops:
  7.2 10.0 %copy-start = (bf16[2,64,2048]{2,1,0:T(8,128)(2,1)S(1)}, bf16[2,64,2048]{2,1,0:T(8,128)(2,1)}, u32[]{:S(2)}) copy-start(bf16[2,64,2048]{2,1,0:T(8,128)(2,1)} %param.19) | copy-start | bytes 1572868
  7.2 18.3 %copy-start.14 = (bf16[2,64,2048]{2,1,0:T(8,128)(2,1)S(1)}, bf16[2,64,2048]{2,1,0:T(8,128)(2,1)}, u32[]{:S(2)}) copy-start(bf16[2,64,2048]{2,1,0:T(8,128)(2,1)} %param.20) | copy-start | bytes 1572868
  9.4 18.1 %copy-start.24 = (f32[2,64,64]{2,1,0:T(8,128)S(1)}, f32[2,64,64]{2,1,0:T(8,128)}, u32[]{:S(2)}) copy-start(f32[2,64,64]{2,1,0:T(8,128)} %param.17) | copy-start | bytes 98308
  9.4 20.4 %copy-start.15 = (bf16[2,64,2048]{2,1,0:T(8,128)(2,1)S(1)}, bf16[2,64,2048]{2,1,0:T(8,128)(2,1)}, u32[]{:S(2)}) copy-start(bf16[2,64,2048]{2,1,0:T(8,128)(2,1)} %param.21) | copy-start | bytes 1572868
  9.4 21.3 %collective-permute-start = (bf16[2,4,1,32,512]{4,3,2,1,0:T(8,128)(2,1)}, bf16[2,4,1,32,512]{4,3,2,1,0:T(8,128)(2,1)S(1)}, u32[]{:S(2)}, u32[]{:S(2)}) collective-permute-start(bf16[2,4,1,32,512]{4,3,2,1,0:T(8,128)(2,1)} %get-tuple-element.233), channel_id=1, source_target_pairs={{0,1},{1,2},{2,3},{3,4},{4,5},{5,6},{6,7},{7,8},{8,9},{9,10},{10,1... | collective-permute-start | bytes 786440 | tf_op jit(solution)/shard_map/ppermute | solution.py:20
  11.4 19.3 %collective-permute-start.1 = (bf16[2,4,1,32,512]{4,3,2,1,0:T(8,128)(2,1)S(1)}, bf16[2,4,1,32,512]{4,3,2,1,0:T(8,128)(2,1)S(1)}, u32[]{:S(2)}, u32[]{:S(2)}) collective-permute-start(bf16[2,4,1,32,512]{4,3,2,1,0:T(8,128)(2,1)S(1)} %get-tuple-element.234), channel_id=1, source_target_pairs={{1,0},{2,1},{3,2},{4,3},{5,4},{6,5},{7,6},{8,7},{9,8},{10,9},{11,1... | collective-permute-start | bytes 786440 | tf_op jit(solution)/shard_map/ppermute | solution.py:21
  18.1 34.5 %all-to-all-start = ((bf16[32,64,128]{2,1,0:T(8,128)(2,1)}), bf16[32,64,128]{2,1,0:T(8,128)(2,1)S(1)}, u32[]{:S(2)}, u32[]{:S(2)}) async-start(bf16[32,64,128]{2,1,0:T(8,128)(2,1)} %bitcast.9), calls=%async_computation | async-start | bytes 1048576 | tf_op jit(solution)/shard_map/all_to_all | solution.py:129
  33.3 5.8 %copy-start.13 = (bf16[27,512,32]{1,2,0:T(8,128)(2,1)S(1)}, bf16[27,512,32]{1,2,0:T(8,128)(2,1)}, u32[]{:S(2)}) copy-start(bf16[27,512,32]{1,2,0:T(8,128)(2,1)} %param.15) | copy-start | bytes 2654212
  53.4 21.7 %all-to-all-start.1 = ((bf16[32,64,128]{2,1,0:T(8,128)(2,1)}), bf16[32,64,128]{2,1,0:T(8,128)(2,1)S(1)}, u32[]{:S(2)}, u32[]{:S(2)}) async-start(bf16[32,64,128]{2,1,0:T(8,128)(2,1)} %bitcast.363), calls=%async_computation.1 | async-start | bytes 1048576 | tf_op jit(solution)/shard_map/all_to_all | solution.py:132
  75.1 22.3 %all-to-all-start.2 = ((bf16[32,64,128]{2,1,0:T(8,128)(2,1)}), bf16[32,64,128]{2,1,0:T(8,128)(2,1)}, u32[]{:S(2)}, u32[]{:S(2)}) async-start(bf16[32,64,128]{2,1,0:T(8,128)(2,1)} %bitcast.362), calls=%async_computation.2 | async-start | bytes 1048576 | tf_op jit(solution)/shard_map/all_to_all | solution.py:135
  85.7 4.3 copy-start.9
  98.3 37.3 %copy-start.8 = (bf16[2,4,2,32,512]{4,3,2,1,0:T(8,128)(2,1)S(1)}, bf16[2,4,2,32,512]{4,3,2,1,0:T(8,128)(2,1)}, u32[]{:S(2)}) copy-start(bf16[2,4,2,32,512]{4,3,2,1,0:T(8,128)(2,1)} %get-tuple-element.215) | copy-start | bytes 1572868
  98.3 38.4 %copy-start.12 = (bf16[2,4,2,32,512]{4,3,2,1,0:T(8,128)(2,1)S(1)}, bf16[2,4,2,32,512]{4,3,2,1,0:T(8,128)(2,1)}, u32[]{:S(2)}) copy-start(bf16[2,4,2,32,512]{4,3,2,1,0:T(8,128)(2,1)} %get-tuple-element.232) | copy-start | bytes 1572868
  127.1 10.6 %copy-start.17 = (f32[512,32]{0,1:T(8,128)S(1)}, f32[512,32]{0,1:T(8,128)}, u32[]{:S(2)}) copy-start(f32[512,32]{0,1:T(8,128)} %fusion.103) | copy-start | bytes 196612
  127.1 10.7 %copy-start.18 = (f32[512,32]{0,1:T(8,128)S(1)}, f32[512,32]{0,1:T(8,128)}, u32[]{:S(2)}) copy-start(f32[512,32]{0,1:T(8,128)} %fusion.105) | copy-start | bytes 196612
  127.1 10.7 %copy-start.19 = (f32[512,32]{0,1:T(8,128)S(1)}, f32[512,32]{0,1:T(8,128)}, u32[]{:S(2)}) copy-start(f32[512,32]{0,1:T(8,128)} %fusion.107) | copy-start | bytes 196612
  127.1 10.7 %copy-start.20 = (f32[512,32]{0,1:T(8,128)S(1)}, f32[512,32]{0,1:T(8,128)}, u32[]{:S(2)}) copy-start(f32[512,32]{0,1:T(8,128)} %fusion.109) | copy-start | bytes 196612
  127.1 12.4 %copy-start.7 = (bf16[2,4,2,32,512]{4,3,2,1,0:T(8,128)(2,1)S(1)}, bf16[2,4,2,32,512]{4,3,2,1,0:T(8,128)(2,1)}, u32[]{:S(2)}) copy-start(bf16[2,4,2,32,512]{4,3,2,1,0:T(8,128)(2,1)} %get-tuple-element.207) | copy-start | bytes 1572868
  127.1 12.4 %copy-start.25 = (f32[32]{0:T(128)S(1)}, f32[32]{0:T(128)}, u32[]{:S(2)}) copy-start(f32[32]{0:T(128)} %param.16) | copy-start | bytes 388
  127.1 22.0 %all-to-all-start.3 = ((bf16[32,64,128]{2,1,0:T(8,128)(2,1)}), bf16[32,64,128]{2,1,0:T(8,128)(2,1)S(1)}, u32[]{:S(2)}, u32[]{:S(2)}) async-start(bf16[32,64,128]{2,1,0:T(8,128)(2,1)} %bitcast.19), calls=%async_computation.3 | async-start | bytes 1048576 | tf_op jit(solution)/shard_map/all_to_all | solution.py:148
  135.7 3.9 copy-start.21
  140.6 9.7 %copy-start.16 = (bf16[2048,64]{0,1:T(8,128)(2,1)S(1)}, bf16[2048,64]{0,1:T(8,128)(2,1)}, u32[]{:S(2)}) copy-start(bf16[2048,64]{0,1:T(8,128)(2,1)} %param.22) | copy-start | bytes 786436
  140.6 9.7 %copy-start.26 = (f32[64]{0:T(128)S(1)}, f32[64]{0:T(128)}, u32[]{:S(2)}) copy-start(f32[64]{0:T(128)} %param.23) | copy-start | bytes 772
  140.9 9.8 %copy-start.22 = (f32[2,64,64]{1,2,0:T(8,128)S(1)}, f32[2,64,64]{1,2,0:T(8,128)}, u32[]{:S(2)}) copy-start(f32[2,64,64]{1,2,0:T(8,128)} %copy.46) | copy-start | bytes 98308
  140.9 9.8 %copy-start.23 = (f32[2,64,64]{1,2,0:T(8,128)S(1)}, f32[2,64,64]{1,2,0:T(8,128)}, u32[]{:S(2)}) copy-start(f32[2,64,64]{1,2,0:T(8,128)} %copy.47) | copy-start | bytes 98308
  152.3 21.9 %all-to-all-start.4 = ((bf16[32,64,128]{2,1,0:T(8,128)(2,1)}), bf16[32,64,128]{2,1,0:T(8,128)(2,1)S(1)}, u32[]{:S(2)}, u32[]{:S(2)}) async-start(bf16[32,64,128]{2,1,0:T(8,128)(2,1)} %bitcast.81), calls=%async_computation.4 | async-start | bytes 1048576 | tf_op jit(solution)/shard_map/all_to_all | solution.py:165
  193.5 3.4 copy-start.3
  219.6 10.7 %copy-start.1 = (f32[2048,1,128]{0,2,1:T(8,128)S(1)}, f32[2048,1,128]{0,2,1:T(8,128)}, u32[]{:S(2)}) copy-start(f32[2048,1,128]{0,2,1:T(8,128)} %get-tuple-element.94) | copy-start | bytes 3145732
  221.9 21.9 %all-to-all-start.7 = ((bf16[32,64,128]{2,1,0:T(8,128)(2,1)}), bf16[32,64,128]{2,1,0:T(8,128)(2,1)S(1)}, u32[]{:S(2)}, u32[]{:S(2)}) async-start(bf16[32,64,128]{2,1,0:T(8,128)(2,1)} %bitcast.90), calls=%async_computation.7 | async-start | bytes 1048576 | tf_op jit(solution)/shard_map/all_to_all | solution.py:214
  230.3 42.9 %copy-start.11 = (bf16[2,64,16,128]{3,2,1,0:T(8,128)(2,1)S(1)}, bf16[2,64,16,128]{3,2,1,0:T(8,128)(2,1)}, u32[]{:S(2)}) copy-start(bf16[2,64,16,128]{3,2,1,0:T(8,128)(2,1)} %copy-done.10) | copy-start | bytes 1572868
  264.7 185.4 %all-to-all-start.5 = ((bf16[32,64,128]{2,1,0:T(8,128)(2,1)}), bf16[32,64,128]{2,1,0:T(8,128)(2,1)S(1)}, u32[]{:S(2)}, u32[]{:S(2)}) async-start(bf16[32,64,128]{2,1,0:T(8,128)(2,1)} %bitcast.368), calls=%async_computation.5 | async-start | bytes 1048576 | tf_op jit(solution)/shard_map/all_to_all | solution.py:212
  273.1 126.0 %reduce-scatter.2.cloned.1.call-start = ((), (), s32[]{:S(2)}) async-start(), calls=%async_computation.9 | async-start | bytes 540672 | tf_op jit(solution)/shard_map/reduce_scatter | solution.py:169
  (11 other events, 17.8 us)
Sparse Core Ops, SparseCore 0:
  277.3 121.8 reduce-scatter.1
